TPU v7x, 128 devices: a whole 4x4x4 slice. The times are simulated.
128 devices in a mesh: cmp: 8 (over z_hi, y), tgt: 16 (over x, z_lo, core).
Axes of the slice: x: 4, y: 4, z: 4 (z_hi: 2, z_lo: 2; z = z_hi * 2 + z_lo), core: 2. Of those that a mesh axis runs over, the one named last changes fastest.
Arguments:
- affinity: bfloat16 [16384, 12288], P('cmp', 'tgt'), may hold values from -6 to 6
- comp_vectors: bfloat16 [16384, 2048], P('cmp'), may hold values from -0.046875 to 0.046875
- targ_vectors: bfloat16 [12288, 2048], P('tgt'), may hold values from -0.0546875 to 0.0546875
- comp_values: float32 [2048], P('cmp'), may hold values from 0.05 to 4
- targ_values: float32 [2048], P('tgt'), may hold values from 0.05 to 4
Outputs:
- predicted: float32 [16384, 12288], P('cmp', 'tgt')
All inputs are finite; a program needn't handle non-finite values.
Results may differ from a plain program's by a relative error of at most 0.0037.
Values may be sent and summed in bfloat16 or wider, within the bound.
A program may use at most 128 MiB of HBM per device.

v0:
```python
import jax
import jax.numpy as jnp
from jax import lax
from jax.sharding import PartitionSpec as P


def shards(affinity, comp_vectors, targ_vectors, comp_values, targ_values):
    vt_cols = targ_vectors
    half_t = lax.psum_scatter(
        lax.dot_general(
            vt_cols, affinity, (((0,), (1,)), ((), ())), preferred_element_type=jnp.float32
        ),
        "tgt",
        scatter_dimension=0,
        tiled=True,
    )
    comp_wide = comp_vectors.astype(jnp.float32)
    vc_cols = comp_wide
    coeffs = lax.psum_scatter(
        lax.dot_general(
            vc_cols,
            half_t,
            (((0,), (1,)), ((), ())),
            precision=lax.Precision.HIGHEST,
            preferred_element_type=jnp.float32,
        ),
        "cmp",
        scatter_dimension=0,
        tiled=True,
    )
    scaled = (coeffs / (comp_values[:, None] * targ_values[None, :] + 0.25)).astype(jnp.bfloat16)
    vc_cols = comp_vectors
    mapped = jnp.dot(
        vc_cols,
        lax.all_gather(scaled, "cmp", axis=0, tiled=True),
        preferred_element_type=jnp.float32,
    ).astype(jnp.bfloat16)
    vt_cols = targ_vectors
    return lax.dot_general(
        lax.all_gather(mapped, "tgt", axis=1, tiled=True),
        vt_cols,
        (((1,), (1,)), ((), ())),
        preferred_element_type=jnp.float32,
    )


def solution(mesh):
    in_specs = (P("cmp", "tgt"), P("cmp", None), P("tgt", None), P("cmp"), P("tgt"))
    out_specs = P("cmp", "tgt")
    return jax.shard_map(shards, mesh=mesh, in_specs=in_specs, out_specs=out_specs, check_vma=False)
```

profile of v0, /device:TPU:0, one launch (start us, length us, event | category | flops | bytes accessed | tf_op | source)
XLA Modules:
  0.0 396.1 jit_solution(5673050714116816492)
XLA Ops:
  6.5 0.0 copy-start
  6.5 0.0 reduce-scatter.3.cloned.1.call-start
  6.5 1.9 copy-done
  8.4 12.1 %fusion.1 = f32[2048,2048]{1,0:T(8,128)} fusion(bf16[768,2048]{1,0:T(8,128)(2,1)S(1)} %copy-done, bf16[2048,768]{1,0:T(8,128)(2,1)} %param.5), kind=kOutput, calls=%fused_computation.4 | convolution fusion | flops 6442450944 | bytes 23068672 | tf_op jit(solution)/shard_map/dot_general | solution.py:10
  20.5 0.0 reduce-scatter.3.cloned.1.call-update
  20.5 0.0 copy-start.1
  20.5 0.0 copy-start.2
  20.5 0.0 reduce-scatter.5.cloned.1.call-start
  20.6 178.2 %reduce-scatter.3.cloned.1.call-done = f32[128,2048]{1,0:T(8,128)} async-done(((f32[2048,2048]{1,0:T(8,128)}), f32[128,2048]{1,0:T(8,128)}) %reduce-scatter.3.cloned.1.call-update) | async-done | bytes 1048592 | tf_op jit(solution)/shard_map/reduce_scatter | solution.py:9
  198.8 8.2 %convolution_bitcast_fusion = f32[2048,128]{0,1:T(8,128)} fusion(f32[128,2048]{1,0:T(8,128)} %reduce-scatter.3.cloned.1.call-done, bf16[2048,2048]{1,0:T(8,128)(2,1)} %param.6), kind=kOutput, calls=%fused_computation | convolution fusion | flops 6442450944 | bytes 10485760 | tf_op jit(solution)/shard_map/dot_general | solution.py:20
  207.0 0.0 reduce-scatter.5.cloned.1.call-update
  207.0 0.0 all-gather.2.cloned.1.call-start
  207.1 77.6 %reduce-scatter.5.cloned.1.call-done = f32[256,128]{0,1:T(8,128)} async-done(((f32[2048,128]{0,1:T(8,128)}), f32[256,128]{0,1:T(8,128)}) %reduce-scatter.5.cloned.1.call-update) | async-done | bytes 131088 | tf_op jit(solution)/shard_map/reduce_scatter | solution.py:19
  284.7 0.0 copy-done.1
  284.7 0.0 copy-done.2
  284.7 1.0 divide_convert_fusion
  285.7 35.1 %all_gather.6 = bf16[2048,128]{0,1:T(8,128)(2,1)S(1)} all-gather(bf16[256,128]{0,1:T(8,128)(2,1)S(1)} %divide_convert_fusion), channel_id=1, replica_groups=mesh['cmp'=8,'tgt'=16] {'cmp'}, dimensions={0}, use_global_device_ids=true | all-gather | bytes 589824 | tf_op jit(solution)/shard_map/all_gather | solution.py:35
  320.8 7.1 %fusion = bf16[2048,128]{0,1:T(8,128)(2,1)} fusion(bf16[2048,128]{0,1:T(8,128)(2,1)S(1)} %all_gather.6, bf16[2048,2048]{1,0:T(8,128)(2,1)} %param.6), kind=kOutput, calls=%fused_computation.2 | convolution fusion | flops 1074003968 | bytes 9437184 | tf_op jit(solution)/shard_map/dot_general | solution.py:33
  327.9 0.0 all-gather.2.cloned.1.call-update
  327.9 50.9 %all-gather.2.cloned.1.call-done = bf16[2048,2048]{0,1:T(8,128)(2,1)} async-done(((bf16[2048,128]{0,1:T(8,128)(2,1)}), bf16[2048,2048]{0,1:T(8,128)(2,1)}) %all-gather.2.cloned.1.call-update) | async-done | bytes 8388624 | tf_op jit(solution)/shard_map/all_gather | solution.py:40
  378.8 10.8 %fusion.2 = f32[2048,768]{1,0:T(8,128)} fusion(bf16[2048,2048]{0,1:T(8,128)(2,1)} %all-gather.2.cloned.1.call-done, bf16[768,2048]{1,0:T(8,128)(2,1)S(1)} %copy-done), kind=kOutput, calls=%fused_computation.5 | convolution fusion | flops 6442450944 | bytes 17825792 | tf_op jit(solution)/shard_map/dot_general | solution.py:39
Async XLA Ops:
  6.5 1.9 copy-start
  6.5 192.3 %reduce-scatter.3.cloned.1.call-start = ((), (), s32[]{:S(2)}) async-start(), calls=%async_computation.2 | async-start | bytes 17825792 | tf_op jit(solution)/shard_map/reduce_scatter | solution.py:9
  20.5 264.1 %copy-start.1 = (f32[256]{0:T(256)S(1)}, f32[256]{0:T(256)}, u32[]{:S(2)}) copy-start(f32[256]{0:T(256)} %param.8) | copy-start | bytes 3076
  20.5 264.1 %copy-start.2 = (f32[128]{0:T(128)S(1)}, f32[128]{0:T(128)}, u32[]{:S(2)}) copy-start(f32[128]{0:T(128)} %param.9) | copy-start | bytes 1540
  20.5 264.1 %reduce-scatter.5.cloned.1.call-start = ((), (), s32[]{:S(2)}) async-start(), calls=%async_computation.3 | async-start | bytes 1179648 | tf_op jit(solution)/shard_map/reduce_scatter | solution.py:19
  207.0 171.7 %all-gather.2.cloned.1.call-start = ((), (), s32[]{:S(2)}) async-start(), calls=%async_computation.4 | async-start | bytes 8912896 | tf_op jit(solution)/shard_map/all_gather | solution.py:40
Sparse Core Ops, SparseCore 0:
  20.6 178.1 reduce-scatter.2
  207.2 77.4 reduce-scatter.4
  328.0 50.7 all-gather.1
where the time goes:
time: 398 us; the launch traced here: 396 us
  waiting for transfers between devices  307 us (77%)
  matrix products  38.2 us (10%)
  blocking collectives  35.1 us (9%)
  between operations  13.1 us (3%)
    reduce_scatter x1, waiting for transfers between devices, shards(): lax.psum_scatter(lax.dot_general(vt_cols, affinity, (((0,), (1,)), ((), (...  178 us
    reduce_scatter x1, waiting for transfers between devices, shards(): lax.psum_scatter(lax.dot_general(vc_cols, half_t, (((0,), (1,)), ((), ())...  77.6 us
    all_gather x1, waiting for transfers between devices, shards(): lax.all_gather(mapped, 'tgt', axis=1, tiled=True)  50.9 us
    all_gather x1, blocking collectives, shards(): lax.all_gather(scaled, 'cmp', axis=0, tiled=True)  35.1 us
    dot_general x1, matrix products, shards(): lax.dot_general(vt_cols, affinity, (((0,), (1,)), ((), ())), preferred_el...  12.1 us
    dot_general x1, matrix products, shards(): lax.dot_general(lax.all_gather(mapped, 'tgt', axis=1, tiled=True), vt_col...  10.8 us
    dot_general x1, matrix products, shards(): lax.dot_general(vc_cols, half_t, (((0,), (1,)), ((), ())), precision=lax....  8.2 us
  transfers between devices with their start and end apart: 3, of which 3 were waited for; matrix products, arithmetic and copies ran while one was open for 0% of the time, Pallas kernels for 0%

commit v1 on v0

v1 whole, which is shorter than its diff:
```python
import functools

import jax
import jax.numpy as jnp
from jax import lax
from jax.experimental import pallas as pl
from jax.experimental.pallas import tpu as pltpu
from jax.sharding import PartitionSpec as P

MESH = pl.DeviceIdType.MESH
F32, BF16 = jnp.float32, jnp.bfloat16
CHUNKS = 2
PARTS = 3
ORDERS = ((1, 2, 4), (2, 4, 1), (4, 1, 2))
ROW_TILE = 512


def flip4(v, bits):
    return (v, v + 1 - 2 * lax.rem(v, 2), 3 - v, lax.rem(v + 2, 4))[bits]


def cmp_at(c, j):
    y = lax.rem(c, 4)
    base = c - y
    return (4 - base if j & 4 else base) + flip4(y, j & 3)


def tgt_at(t, k):
    x, z, core = t // 4, lax.rem(t // 2, 2), lax.rem(t, 2)
    z = 1 - z if k & 4 else z
    core = 1 - core if k & 8 else core
    return flip4(x, k & 3) * 4 + z * 2 + core


def block_of(p, r):
    d1, d2, d3 = ORDERS[p]
    return (d1 if r & 4 else 0) + (d2 if r & 2 else 0) + (d3 if r & 1 else 0)


def dim_of(p, r):
    return ORDERS[p][0 if r & 4 else 1 if r & 2 else 2]


def kernel(
    y_hbm, vc_hbm, vt_hbm, lc_ref, lt_ref, out_hbm,
    y, vc, vct, vt, acc, den, psend, precv, wown, qsend, qown, qrecv, q2send, q2recv, s, tbuf,
    in_sem, out_sem, p_ss, p_rs, c_ss, c_rs, q_ss, q_rs, s_ss, s_rs, d_ss, d_rs, t_ss, t_rs,
):
    c, t = lax.axis_index("cmp"), lax.axis_index("tgt")
    rows, cols = y.shape[1], y.shape[2]
    kb = vc.shape[1] // 8
    kcs = kb // CHUNKS
    tb = vt.shape[1] // 16

    cmp_peer = {d: {"cmp": cmp_at(c, d), "tgt": t} for d in (1, 2, 4)}
    tgt_peer = {k: {"cmp": c, "tgt": tgt_at(t, k)} for k in range(1, 9)}

    def remote(src, dst, ss, rs, peer):
        return pltpu.make_async_remote_copy(
            src_ref=src, dst_ref=dst, send_sem=ss, recv_sem=rs, device_id=peer, device_id_type=MESH
        )

    barrier = pltpu.get_barrier_semaphore()
    for peer in list(cmp_peer.values()) + list(tgt_peer.values()):
        pl.semaphore_signal(barrier, inc=1, device_id=peer, device_id_type=MESH)

    vc_in = [
        pltpu.make_async_copy(
            vc_hbm.at[:, pl.ds(pl.multiple_of(cmp_at(c, j) * kb, kb), kb)],
            vc.at[:, pl.ds(j * kb, kb)],
            in_sem.at[j],
        )
        for j in range(8)
    ]
    y_in = [
        pltpu.make_async_copy(y_hbm.at[:, pl.ds(p * cols, cols)], y.at[p], in_sem.at[8 + p])
        for p in range(PARTS)
    ]
    vt_in = [
        pltpu.make_async_copy(
            vt_hbm.at[:, pl.ds(pl.multiple_of(tgt_at(t, k) * tb, tb), tb)],
            vt.at[:, pl.ds(k * tb, tb)],
            in_sem.at[11 + k],
        )
        for k in range(16)
    ]
    y_in[0].start()
    for j in (7, 3, 5, 1):
        vc_in[j].start()
    y_in[1].start()
    y_in[2].start()
    for j in (6, 2, 4, 0):
        vc_in[j].start()
    for copy in vt_in:
        copy.start()

    def transpose(j):
        vc_in[j].wait()
        vct[pl.ds(j * kb, kb), :] = vc[:, pl.ds(j * kb, kb)].T

    def product(h, p, rs):
        lhs = [vct[pl.ds(block_of(p, r) * kb + h * kcs, kcs), :] for r in rs]
        return jnp.dot(jnp.concatenate(lhs, axis=0), y[p], preferred_element_type=F32)

    def p_copy(h, p, r):
        return remote(
            psend.at[h, p, r - 1], precv.at[h, p, r - 1], p_ss.at[h, p, r - 1], p_rs.at[h, p, r - 1],
            cmp_peer[dim_of(p, r)],
        )

    def got(h, p, r):
        p_copy(h, p, r).wait_recv()
        return precv[h, p, r - 1].astype(F32)

    def p1_compute(h, p):
        prod = product(h, p, (7, 6, 5, 4))
        for i, r in enumerate((7, 6, 5, 4)):
            psend[h, p, r - 1] = prod[i * kcs : (i + 1) * kcs].astype(BF16)

    def p1_send(h, p, rs=(7, 6, 5, 4)):
        for r in rs:
            p_copy(h, p, r).start()

    def p2(h, p):
        prod = product(h, p, (3, 2))
        for i, r in enumerate((3, 2)):
            psend[h, p, r - 1] = (prod[i * kcs : (i + 1) * kcs] + got(h, p, r + 4)).astype(BF16)
            p_copy(h, p, r).start()

    def p3(h, p):
        prod = product(h, p, (1, 0))
        wown[h, p] = prod[kcs:]
        psend[h, p, 0] = (prod[:kcs] + got(h, p, 5) + got(h, p, 3)).astype(BF16)
        p_copy(h, p, 1).start()

    def c_copy(h):
        return remote(qsend.at[h], qrecv.at[h], c_ss.at[h], c_rs.at[h], tgt_peer[8])

    def pf(h):
        w = jnp.concatenate(
            [wown[h, p] + got(h, p, 4) + got(h, p, 2) + got(h, p, 1) for p in range(PARTS)], axis=1
        )
        high = w.astype(BF16)
        low = (w - high.astype(F32)).astype(BF16)
        both = jnp.concatenate([high, low], axis=0)
        for k in list(range(8, 16)) + list(range(8)):
            if k % 2:
                continue
            q = jnp.dot(both, vt[:, k * tb : (k + 2) * tb], preferred_element_type=F32)
            q = q[:kcs] + q[kcs:]
            for i in range(2):
                block = q[:, i * tb : (i + 1) * tb]
                if k >= 8:
                    qsend[h, k - 8 + i] = block
                else:
                    qown[h, k + i] = block
            if k == 14:
                c_copy(h).start()

    def q_copy(h, k):
        return remote(q2send.at[h, k - 1], q2recv.at[h, k - 1], q_ss.at[h, k - 1], q_rs.at[h, k - 1], tgt_peer[k])

    def m1(h):
        c_copy(h).wait_recv()
        for k in (3, 7, 1, 2, 5, 6, 4):
            q2send[h, k - 1] = qown[h, k] + qrecv[h, k]
            q_copy(h, k).start()

    def s_copy(h, k):
        return remote(s.at[h, 0, 0], s.at[h, 0, k], s_ss.at[h, k - 1], s_rs.at[h, k - 1], tgt_peer[k])

    def m2(h):
        total = qown[h, 0] + qrecv[h, 0]
        for k in range(1, 8):
            q_copy(h, k).wait_recv()
            total += q2recv[h, k - 1]
        s[h, 0, 0] = (total / den[h * kcs : (h + 1) * kcs, :]).astype(BF16)
        for k in (3, 7, 1, 2, 5, 6, 4):
            s_copy(h, k).start()

    def d_copy(h):
        return remote(s.at[h, 0], s.at[h, 1], d_ss.at[h], d_rs.at[h], tgt_peer[8])

    def m3(h):
        for k in range(1, 8):
            s_copy(h, k).wait_recv()
        d_copy(h).start()

    def t_copy(h, p, r):
        d = 4 if r & 4 else 2 if r & 2 else 1
        return remote(
            tbuf.at[h, p, r - d], tbuf.at[h, p, r], t_ss.at[h, p, r - 1], t_rs.at[h, p, r - 1],
            cmp_peer[dim_of(p, r)],
        )

    def m4(h):
        d_copy(h).wait_recv()
        lhs = jnp.concatenate([s[h, i, k] for i in range(2) for k in range(8)], axis=1)
        for p in range(PARTS):
            part = lax.dot_general(
                lhs, vt[p * cols : (p + 1) * cols, :], (((1,), (1,)), ((), ())), preferred_element_type=F32
            )
            tbuf[h, p, 0] = part.astype(BF16)
            for r in (4, 2, 1):
                t_copy(h, p, r).start()

    def a1(h):
        for p in range(PARTS):
            t_copy(h, p, 1).wait_recv()
            t_copy(h, p, 3).start()
            t_copy(h, p, 5).start()
            t_copy(h, p, 2).wait_recv()
            t_copy(h, p, 6).start()

    def a2(h):
        for p in range(PARTS):
            t_copy(h, p, 3).wait_recv()
            t_copy(h, p, 7).start()

    def o_copy(p, i):
        start = pl.multiple_of(i * ROW_TILE, ROW_TILE)
        return pltpu.make_async_copy(
            acc.at[p, pl.ds(start, ROW_TILE)],
            out_hbm.at[pl.ds(start, ROW_TILE), pl.ds(p * cols, cols)],
            out_sem.at[p, i],
        )

    def accumulate(h, group, first, last):
        for p in range(PARTS):
            for r in group:
                if r in (4, 5, 6, 7):
                    t_copy(h, p, r).wait_recv()
            rhs = jnp.concatenate([tbuf[h, p, r] for r in group], axis=0)

            @pl.loop(0, rows // ROW_TILE)
            def _(i):
                at = pl.ds(pl.multiple_of(i * ROW_TILE, ROW_TILE), ROW_TILE)
                lhs = jnp.concatenate(
                    [vc[at, pl.ds(block_of(p, r) * kb + h * kcs, kcs)] for r in group], axis=1
                )
                prod = jnp.dot(lhs, rhs, preferred_element_type=F32)
                acc[p, at, :] = prod if first else acc[p, at, :] + prod
                if last:
                    o_copy(p, i).start()

    y_in[0].wait()
    for j in (7, 3, 5, 1):
        transpose(j)
    p1_compute(0, 0)
    pl.semaphore_wait(barrier, len(cmp_peer) + len(tgt_peer))
    p1_send(0, 0)
    transpose(6)
    transpose(2)
    y_in[1].wait()
    p1_compute(0, 1)
    p1_send(0, 1)
    transpose(4)
    y_in[2].wait()
    p1_compute(0, 2)
    p1_send(0, 2)
    transpose(0)
    den[...] = (
        jnp.broadcast_to(lc_ref[...], (tb, kb)).T * jnp.broadcast_to(lt_ref[...], (kb, tb)) + 0.25
    )
    for copy in vt_in:
        copy.wait()

    for p in range(PARTS):
        p1_compute(1, p)
    for p in range(PARTS):
        p2(0, p)
    for p in range(PARTS):
        p1_send(1, p, (7, 6))
    for p in range(PARTS):
        p3(0, p)
    for p in range(PARTS):
        p1_send(1, p, (5, 4))
    pf(0)
    for p in range(PARTS):
        p2(1, p)
    m1(0)
    for p in range(PARTS):
        p3(1, p)
    m2(0)
    pf(1)
    m3(0)
    m1(1)
    m4(0)
    m2(1)
    a1(0)
    m3(1)
    a2(0)
    m4(1)
    accumulate(0, (0, 1, 2, 4), True, False)
    a1(1)
    a2(1)
    accumulate(0, (3, 5, 6, 7), False, False)
    accumulate(1, (0, 1, 2, 4), False, False)
    accumulate(1, (3, 5, 6, 7), False, True)

    for h in range(CHUNKS):
        c_copy(h).wait_send()
        d_copy(h).wait_send()
        for r in range(1, 8):
            q_copy(h, r).wait_send()
            s_copy(h, r).wait_send()
            for p in range(PARTS):
                p_copy(h, p, r).wait_send()
                t_copy(h, p, r).wait_send()
    for p in range(PARTS):
        for i in range(rows // ROW_TILE):
            o_copy(p, i).wait()


def shards(affinity, comp_vectors, targ_vectors, comp_values, targ_values):
    rows, targets = affinity.shape
    kc, kt = comp_vectors.shape[1], targ_vectors.shape[1]
    cols, kb, tb = targets // PARTS, kc // 8, kt // 16
    n, kcs = CHUNKS, kb // CHUNKS
    any_space = pl.BlockSpec(memory_space=pl.ANY)
    vmem = pl.BlockSpec(memory_space=pltpu.VMEM)
    dma = pltpu.SemaphoreType.DMA
    return pl.pallas_call(
        kernel,
        out_shape=jax.ShapeDtypeStruct((rows, targets), F32),
        in_specs=[any_space, any_space, any_space, vmem, vmem],
        out_specs=any_space,
        scratch_shapes=[
            pltpu.VMEM((PARTS, rows, cols), BF16),
            pltpu.VMEM((rows, kc), BF16),
            pltpu.VMEM((kc, rows), BF16),
            pltpu.VMEM((targets, kt), BF16),
            pltpu.VMEM((PARTS, rows, cols), F32),
            pltpu.VMEM((kb, tb), F32),
            pltpu.VMEM((n, PARTS, 7, kcs, cols), BF16),
            pltpu.VMEM((n, PARTS, 7, kcs, cols), BF16),
            pltpu.VMEM((n, PARTS, kcs, cols), F32),
            pltpu.VMEM((n, 8, kcs, tb), F32),
            pltpu.VMEM((n, 8, kcs, tb), F32),
            pltpu.VMEM((n, 8, kcs, tb), F32),
            pltpu.VMEM((n, 7, kcs, tb), F32),
            pltpu.VMEM((n, 7, kcs, tb), F32),
            pltpu.VMEM((n, 2, 8, kcs, tb), BF16),
            pltpu.VMEM((n, PARTS, 8, kcs, cols), BF16),
            dma((27,)),
            dma((PARTS, rows // ROW_TILE)),
            dma((n, PARTS, 7)),
            dma((n, PARTS, 7)),
            dma((n,)),
            dma((n,)),
            dma((n, 7)),
            dma((n, 7)),
            dma((n, 7)),
            dma((n, 7)),
            dma((n,)),
            dma((n,)),
            dma((n, PARTS, 7)),
            dma((n, PARTS, 7)),
        ],
        compiler_params=pltpu.CompilerParams(
            collective_id=0, has_side_effects=True, vmem_limit_bytes=60 << 20
        ),
    )(affinity, comp_vectors, targ_vectors, comp_values[None, :], targ_values[None, :])


def solution(mesh):
    in_specs = (P("cmp", "tgt"), P("cmp", None), P("tgt", None), P("cmp"), P("tgt"))
    out_specs = P("cmp", "tgt")
    return jax.shard_map(shards, mesh=mesh, in_specs=in_specs, out_specs=out_specs, check_vma=False)
```

time: 398 us -> 94.6 us (0.24)
  waiting for transfers between devices: 307 us -> 0 us
  Pallas kernels: 0 us -> 88.5 us
  matrix products: 38.2 us -> 0 us
  blocking collectives: 35.1 us -> 0 us
  between operations: 13.1 us -> 0.01 us
  local copies, waits for them, and re-layouts: 1.9 us -> 5.89 us
    reduce_scatter x2 -> x0, waiting for transfers between devices: 256 us -> none  [the longest x1 178 us: shards(): lax.psum_scatter(lax.dot_general(vt_cols, affinity, (((0,), (1,)), ((), (...]
    pallas_call x0 -> x1, Pallas kernels: none -> 88.5 us  [shards(): pl.pallas_call(kernel, out_shape=jax.ShapeDtypeStruct((rows, targets), F3...]
    all_gather x1 -> x0, waiting for transfers between devices: 50.9 us -> none  [shards(): lax.all_gather(mapped, 'tgt', axis=1, tiled=True)]
    dot_general x4 -> x0, matrix products: 38.2 us -> none  [the longest x1 12.1 us: shards(): lax.dot_general(vt_cols, affinity, (((0,), (1,)), ((), ())), preferred_el...]
    all_gather x1 -> x0, blocking collectives: 35.1 us -> none  [shards(): lax.all_gather(scaled, 'cmp', axis=0, tiled=True)]
    unnamed x6 -> x1, local copies, waits for them, and re-layouts: 1.9 us -> 5.89 us
  transfers between devices with their start and end apart: 3 -> 0, of which waited for: 3 -> 0; matrix products, arithmetic and copies ran while one was open for 0% -> 0% of each run, Pallas kernels for 0% -> 0%
where the time goes in v1:
time: 94.6 us; the launch traced here: 94.4 us
  Pallas kernels  88.5 us (94%)
  local copies, waits for them, and re-layouts  5.89 us (6%)
    pallas_call x1, Pallas kernels, shards(): pl.pallas_call(kernel, out_shape=jax.ShapeDtypeStruct((rows, targets), F3...  88.5 us
    unnamed x1, local copies, waits for them, and re-layouts  5.89 us

profile of v1, /device:TPU:0, one launch (start us, length us, event | category | flops | bytes accessed | tf_op | source)
XLA Modules:
  0.0 94.4 jit_solution(16944073911687867461)
XLA Ops:
  0.0 88.5 %shard_map.55 = f32[2048,768]{1,0:T(8,128)} custom-call(bf16[2048,768]{1,0:T(8,128)(2,1)} %y_hbm.1, bf16[2048,2048]{1,0:T(8,128)(2,1)} %vc_hbm.1, bf16[768,2048]{1,0:T(8,128)(2,1)} %vt_hbm.1, f32[1,256]{1,0:T(1,128)} %bitcast.2, f32[1,128]{1,0:T(1,128)} %bitcast.3), custom_call_target="tpu_custom_call" | custom-call | tf_op jit(solution)/shard_map/pallas_call | solution.py:323
  88.5 5.9 %copy.7 = f32[2048,768]{1,0:T(8,128)} copy(f32[2048,768]{1,0:T(8,128)} %shard_map.55) | data formatting | bytes 12582912

commit v2 on v1

v2 whole, which is shorter than its diff:
```python
import functools

import jax
import jax.numpy as jnp
from jax import lax
from jax.experimental import pallas as pl
from jax.experimental.pallas import tpu as pltpu
from jax.sharding import PartitionSpec as P

MESH = pl.DeviceIdType.MESH
F32, BF16 = jnp.float32, jnp.bfloat16
CHUNKS = 4
PARTS = 3
SUM_DIMS = ((1, 2, 4), (2, 1, 4), (4, 1, 2))
GATHER_DIMS = ((1, 2, 4), (2, 1, 4), (4, 2, 1))
ROW_TILE = 512
STEPS = (
    ("ps", 0, 2), ("tr", 6), ("tr", 5), ("tr", 2), ("ps", 0, 0), ("ps", 0, 1), ("pt", 0, 0), ("pc", 1, 0),
    ("ps", 1, 0), ("pt", 0, 1), ("pc", 1, 1), ("pc", 1, 2), ("ps", 1, 1), ("ps", 1, 2), ("tr", 3), ("tr", 0),
    ("pt", 1, 2), ("p2", 0, 1), ("p2", 0, 0), ("tr", 1), ("tr", 4), ("tr", 7), ("pt", 1, 0), ("pt", 0, 2),
    ("p2", 0, 2), ("pc", 3, 1), ("p2", 1, 0), ("pc", 2, 0), ("pt", 1, 1), ("p3", 0, 0), ("p3", 0, 1), ("p2", 1, 1),
    ("p2", 1, 2), ("setup",), ("p3", 0, 2), ("pc", 3, 0), ("p3", 1, 0), ("ps", 3, 0), ("pt", 3, 0), ("ps", 3, 1),
    ("p3", 1, 1), ("pc", 2, 1), ("ps", 2, 0), ("pc", 3, 2), ("ps", 3, 2), ("pt", 3, 2), ("p3", 1, 2), ("ps", 2, 1),
    ("pf", 0), ("p2", 3, 0), ("pt", 2, 0), ("pc", 2, 2), ("ps", 2, 2), ("pt", 3, 1), ("m1", 0), ("p2", 3, 1),
    ("pf", 1), ("p2", 2, 0), ("p2", 3, 2), ("pt", 2, 2), ("pt", 2, 1), ("m1", 1), ("p2", 2, 1), ("p3", 3, 0),
    ("p3", 3, 1), ("m2", 0), ("p2", 2, 2), ("p3", 2, 0), ("p3", 3, 2), ("p3", 2, 1), ("m2", 1), ("m3", 0),
    ("p3", 2, 2), ("pf", 3), ("m3", 1), ("m1", 3), ("m5", 0), ("pf", 2), ("m6", 0), ("m5", 1), ("m1", 2), ("m2", 3),
    ("m6", 1), ("m2", 2), ("a1", 0, 0), ("a1", 0, 1), ("m3", 3), ("a1", 1, 0), ("m3", 2), ("a1", 0, 2), ("a1", 1, 1),
    ("acc", 0, 0, 1), ("m5", 3), ("a1", 1, 2), ("a2", 0, 0), ("a2", 0, 1), ("a2", 1, 0), ("acc", 0, 0, 0),
    ("a2", 1, 1), ("m6", 3), ("m5", 2), ("acc", 0, 0, 2), ("m6", 2), ("a2", 1, 2), ("a1", 3, 0), ("a2", 0, 2),
    ("a1", 3, 2), ("acc", 0, 1, 0), ("acc", 0, 1, 1), ("a1", 2, 0), ("a1", 2, 2), ("a1", 3, 1), ("a1", 2, 1),
    ("acc", 1, 0, 1), ("acc", 1, 0, 2), ("a2", 3, 0), ("a2", 3, 2), ("a2", 2, 0), ("a2", 2, 2), ("a2", 3, 1),
    ("acc", 1, 0, 0), ("a2", 2, 1), ("acc", 0, 1, 2), ("acc", 1, 1, 0), ("acc", 1, 1, 2), ("acc", 1, 1, 1),)


def flip4(v, bits):
    return (v, v + 1 - 2 * lax.rem(v, 2), 3 - v, lax.rem(v + 2, 4))[bits]


def cmp_at(c, j):
    y = lax.rem(c, 4)
    base = c - y
    return (4 - base if j & 4 else base) + flip4(y, j & 3)


def tgt_at(t, k):
    x, z, core = t // 4, lax.rem(t // 2, 2), lax.rem(t, 2)
    z = 1 - z if k & 4 else z
    core = 1 - core if k & 8 else core
    return flip4(x, k & 3) * 4 + z * 2 + core


def block_of(dims, r):
    return (dims[0] if r & 4 else 0) + (dims[1] if r & 2 else 0) + (dims[2] if r & 1 else 0)


def dim_of(dims, r):
    return dims[0 if r & 4 else 1 if r & 2 else 2]


def kernel(
    y_hbm, vc_hbm, vt_hbm, lc_ref, lt_ref, out_hbm,
    y, vc, vct, vt, vtt, acc, den, psend, precv, wown, qsend, qown, qrecv, q2send, q2recv, s, tbuf,
    in_sem, out_sem, p_ss, p_rs, c_ss, c_rs, q_ss, q_rs, s_ss, s_rs, d_ss, d_rs, t_ss, t_rs,
):
    c, t = lax.axis_index("cmp"), lax.axis_index("tgt")
    rows, cols = y.shape[1], y.shape[2]
    kb = vc.shape[1] // 8
    kcs = kb // CHUNKS
    half = kb // 2
    tb = vt.shape[1] // 16

    cmp_peer = {d: {"cmp": cmp_at(c, d), "tgt": t} for d in (1, 2, 4)}
    tgt_peer = {k: {"cmp": c, "tgt": tgt_at(t, k)} for k in range(1, 9)}

    def remote(src, dst, ss, rs, peer):
        return pltpu.make_async_remote_copy(
            src_ref=src, dst_ref=dst, send_sem=ss, recv_sem=rs, device_id=peer, device_id_type=MESH
        )

    barrier = pltpu.get_barrier_semaphore()
    for peer in list(cmp_peer.values()) + list(tgt_peer.values()):
        pl.semaphore_signal(barrier, inc=1, device_id=peer, device_id_type=MESH)

    vc_in = {}
    for i in range(2):
        for j in range(8):
            vc_in[i, j] = pltpu.make_async_copy(
                vc_hbm.at[:, pl.ds(pl.multiple_of(cmp_at(c, j) * kb + i * half, half), half)],
                vc.at[:, pl.ds(j * kb + i * half, half)],
                in_sem.at[i * 8 + j],
            )
    y_in = [
        pltpu.make_async_copy(y_hbm.at[:, pl.ds(p * cols, cols)], y.at[p], in_sem.at[16 + p])
        for p in range(PARTS)
    ]
    vt_in = [
        pltpu.make_async_copy(
            vt_hbm.at[:, pl.ds(pl.multiple_of(tgt_at(t, k) * tb, tb), tb)],
            vt.at[:, pl.ds(k * tb, tb)],
            in_sem.at[19 + k],
        )
        for k in range(16)
    ]
    load_order = (7, 3, 5, 1, 6, 2, 4, 0)
    for j in load_order[:4]:
        vc_in[0, j].start()
    y_in[0].start()
    for j in load_order[4:]:
        vc_in[0, j].start()
    y_in[1].start()
    y_in[2].start()
    for j in load_order:
        vc_in[1, j].start()
    for copy in vt_in:
        copy.start()

    def transpose(i, js):
        for j in js:
            vc_in[i, j].wait()
            at = pl.ds(j * kb + i * half, half)
            vct[at, :] = vc[:, at].T

    def p_copy(h, p, r):
        return remote(
            psend.at[h, p, r - 1], precv.at[h, p, r - 1], p_ss.at[h, p, r - 1], p_rs.at[h, p, r - 1],
            cmp_peer[dim_of(SUM_DIMS[p], r)],
        )

    def got(h, p, r):
        p_copy(h, p, r).wait_recv()
        return precv[h, p, r - 1].astype(F32)

    def pc(h, p):
        lhs = [
            vct[pl.ds(block_of(SUM_DIMS[p], r) * kb + h * kcs, kcs), :] for r in range(7, -1, -1)
        ]
        prod = jnp.dot(jnp.concatenate(lhs, axis=0), y[p], preferred_element_type=F32)
        for i, r in enumerate(range(7, -1, -1)):
            block = prod[i * kcs : (i + 1) * kcs]
            if r >= 4:
                psend[h, p, r - 1] = block.astype(BF16)
            else:
                wown[h, p, r] = block

    def ps(h, p):
        p_copy(h, p, 7).start()
        p_copy(h, p, 6).start()

    def pt(h, p):
        p_copy(h, p, 5).start()
        p_copy(h, p, 4).start()

    def p2(h, p):
        for r in (3, 2):
            psend[h, p, r - 1] = (wown[h, p, r] + got(h, p, r + 4)).astype(BF16)
            p_copy(h, p, r).start()

    def p3(h, p):
        psend[h, p, 0] = (wown[h, p, 1] + got(h, p, 5) + got(h, p, 3)).astype(BF16)
        p_copy(h, p, 1).start()

    def c_copy(h):
        return remote(qsend.at[h], qrecv.at[h], c_ss.at[h], c_rs.at[h], tgt_peer[8])

    def pf(h):
        w = jnp.concatenate(
            [wown[h, p, 0] + got(h, p, 4) + got(h, p, 2) + got(h, p, 1) for p in range(PARTS)], axis=1
        )
        high = w.astype(BF16)
        low = (w - high.astype(F32)).astype(BF16)
        both = jnp.concatenate([high, low], axis=0)
        for k in (8, 10, 12, 14, 0, 2, 4, 6):
            q = jnp.dot(both, vt[:, k * tb : (k + 2) * tb], preferred_element_type=F32)
            q = q[:kcs] + q[kcs:]
            for i in range(2):
                block = q[:, i * tb : (i + 1) * tb]
                if k >= 8:
                    qsend[h, k - 8 + i] = block
                else:
                    qown[h, k + i] = block
            if k == 14:
                c_copy(h).start()

    def q_copy(h, k):
        if k == 4:
            return remote(q2send.at[h, 3], q2recv.at[h, 3], q_ss.at[h, 3], q_rs.at[h, 3], tgt_peer[4])
        return remote(q2send.at[h, k - 1], q2recv.at[h, k - 1], q_ss.at[h, k - 1], q_rs.at[h, k - 1], tgt_peer[k & 3])

    def m1(h):
        c_copy(h).wait_recv()
        for k in (7, 3, 5, 6, 1, 2):
            q2send[h, k - 1] = qown[h, k] + qrecv[h, k]
            q_copy(h, k).start()

    def m2(h):
        total = qown[h, 4] + qrecv[h, 4]
        for k in (5, 6, 7):
            q_copy(h, k).wait_recv()
            total += q2recv[h, k - 1]
        q2send[h, 3] = total
        q_copy(h, 4).start()
        total = qown[h, 0] + qrecv[h, 0]
        for k in (1, 2, 3):
            q_copy(h, k).wait_recv()
            total += q2recv[h, k - 1]
        qown[h, 0] = total

    def s_copy(h, k):
        return remote(s.at[h, 0, 0], s.at[h, 0, k], s_ss.at[h, k - 1], s_rs.at[h, k - 1], tgt_peer[k])

    def m3(h):
        q_copy(h, 4).wait_recv()
        total = qown[h, 0] + q2recv[h, 3]
        s[h, 0, 0] = (total / den[h * kcs : (h + 1) * kcs, :]).astype(BF16)
        for k in (7, 3, 5, 6, 1, 2, 4):
            s_copy(h, k).start()

    def d_copy(h):
        return remote(s.at[h, 0], s.at[h, 1], d_ss.at[h], d_rs.at[h], tgt_peer[8])

    def m5(h):
        for k in range(1, 8):
            s_copy(h, k).wait_recv()
        d_copy(h).start()

    def t_copy(h, p, r):
        d = 4 if r & 4 else 2 if r & 2 else 1
        return remote(
            tbuf.at[h, p, r - d], tbuf.at[h, p, r], t_ss.at[h, p, r - 1], t_rs.at[h, p, r - 1],
            cmp_peer[dim_of(GATHER_DIMS[p], r)],
        )

    def m6(h):
        d_copy(h).wait_recv()
        lhs = jnp.concatenate([s[h, i, k] for i in range(2) for k in range(8)], axis=1)
        part = jnp.dot(lhs, vtt[...], preferred_element_type=F32).astype(BF16)
        for p in range(PARTS):
            tbuf[h, p, 0] = part[:, p * cols : (p + 1) * cols]
        for r in (1, 2, 4):
            for p in range(PARTS):
                t_copy(h, p, r).start()

    def a1(h, p):
        t_copy(h, p, 1).wait_recv()
        t_copy(h, p, 2).wait_recv()
        for r in (3, 5, 6):
            t_copy(h, p, r).start()

    def a2(h, p):
        t_copy(h, p, 3).wait_recv()
        t_copy(h, p, 7).start()

    def o_copy(p, i):
        start = pl.multiple_of(i * ROW_TILE, ROW_TILE)
        return pltpu.make_async_copy(
            acc.at[p, pl.ds(start, ROW_TILE)],
            out_hbm.at[pl.ds(start, ROW_TILE), pl.ds(p * cols, cols)],
            out_sem.at[p, i],
        )

    per_half = CHUNKS // 2

    def acc_step(i, far, p):
        chunks = range(i * per_half, (i + 1) * per_half)
        group = (3, 5, 6, 7) if far else (0, 1, 2, 4)
        first, last = not (i or far), i and far
        for h in chunks:
            for r in group:
                if r >= 4:
                    t_copy(h, p, r).wait_recv()
        rhs = jnp.concatenate([tbuf[h, p, r] for r in group for h in chunks], axis=0)

        @pl.loop(0, rows // ROW_TILE)
        def _(n):
            at = pl.ds(pl.multiple_of(n * ROW_TILE, ROW_TILE), ROW_TILE)
            lhs = jnp.concatenate(
                [vc[at, pl.ds(block_of(GATHER_DIMS[p], r) * kb + i * half, half)] for r in group], axis=1
            )
            prod = jnp.dot(lhs, rhs, preferred_element_type=F32)
            acc[p, at, :] = prod if first else acc[p, at, :] + prod
            if last:
                o_copy(p, n).start()

    def setup():
        den[...] = (
            jnp.broadcast_to(lc_ref[...], (tb, kb)).T * jnp.broadcast_to(lt_ref[...], (kb, tb)) + 0.25
        )
        for copy in vt_in:
            copy.wait()
        vtt[...] = vt[...].T

    transpose(0, load_order)
    for p in range(PARTS):
        y_in[p].wait()
        pc(0, p)
    pl.semaphore_wait(barrier, len(cmp_peer) + len(tgt_peer))

    steps = {
        "tr": lambda n: transpose(1, (load_order[n],)), "setup": setup, "pc": pc, "ps": ps, "pt": pt,
        "p2": p2, "p3": p3, "pf": pf, "m1": m1, "m2": m2, "m3": m3, "m5": m5, "m6": m6, "a1": a1,
        "a2": a2, "acc": acc_step,
    }
    for name, *where in STEPS:
        steps[name](*where)

    for h in range(CHUNKS):
        c_copy(h).wait_send()
        d_copy(h).wait_send()
        for r in range(1, 8):
            q_copy(h, r).wait_send()
            s_copy(h, r).wait_send()
            for p in range(PARTS):
                p_copy(h, p, r).wait_send()
                t_copy(h, p, r).wait_send()
    for p in range(PARTS):
        for i in range(rows // ROW_TILE):
            o_copy(p, i).wait()


def shards(affinity, comp_vectors, targ_vectors, comp_values, targ_values):
    rows, targets = affinity.shape
    kc, kt = comp_vectors.shape[1], targ_vectors.shape[1]
    cols, kb, tb = targets // PARTS, kc // 8, kt // 16
    n, kcs = CHUNKS, kb // CHUNKS
    any_space = pl.BlockSpec(memory_space=pl.ANY)
    vmem = pl.BlockSpec(memory_space=pltpu.VMEM)
    dma = pltpu.SemaphoreType.DMA
    return pl.pallas_call(
        kernel,
        out_shape=jax.ShapeDtypeStruct((rows, targets), F32),
        in_specs=[any_space, any_space, any_space, vmem, vmem],
        out_specs=any_space,
        scratch_shapes=[
            pltpu.VMEM((PARTS, rows, cols), BF16),
            pltpu.VMEM((rows, kc), BF16),
            pltpu.VMEM((kc, rows), BF16),
            pltpu.VMEM((targets, kt), BF16),
            pltpu.VMEM((kt, targets), BF16),
            pltpu.VMEM((PARTS, rows, cols), F32),
            pltpu.VMEM((kb, tb), F32),
            pltpu.VMEM((n, PARTS, 7, kcs, cols), BF16),
            pltpu.VMEM((n, PARTS, 7, kcs, cols), BF16),
            pltpu.VMEM((n, PARTS, 4, kcs, cols), F32),
            pltpu.VMEM((n, 8, kcs, tb), F32),
            pltpu.VMEM((n, 8, kcs, tb), F32),
            pltpu.VMEM((n, 8, kcs, tb), F32),
            pltpu.VMEM((n, 7, kcs, tb), F32),
            pltpu.VMEM((n, 7, kcs, tb), F32),
            pltpu.VMEM((n, 2, 8, kcs, tb), BF16),
            pltpu.VMEM((n, PARTS, 8, kcs, cols), BF16),
            dma((35,)),
            dma((PARTS, rows // ROW_TILE)),
            dma((n, PARTS, 7)),
            dma((n, PARTS, 7)),
            dma((n,)),
            dma((n,)),
            dma((n, 7)),
            dma((n, 7)),
            dma((n, 7)),
            dma((n, 7)),
            dma((n,)),
            dma((n,)),
            dma((n, PARTS, 7)),
            dma((n, PARTS, 7)),
        ],
        compiler_params=pltpu.CompilerParams(
            collective_id=0, has_side_effects=True, vmem_limit_bytes=60 << 20
        ),
    )(affinity, comp_vectors, targ_vectors, comp_values[None, :], targ_values[None, :])


def solution(mesh):
    in_specs = (P("cmp", "tgt"), P("cmp", None), P("tgt", None), P("cmp"), P("tgt"))
    out_specs = P("cmp", "tgt")
    return jax.shard_map(shards, mesh=mesh, in_specs=in_specs, out_specs=out_specs, check_vma=False)
```

time: 94.6 us -> 85.4 us (0.903)
  Pallas kernels: 88.5 us -> 79.3 us
    pallas_call x1, Pallas kernels: 88.5 us -> 79.3 us  [shards(): pl.pallas_call(kernel, out_shape=jax.ShapeDtypeStruct((rows, targets), F3...]
where the time goes in v2:
time: 85.4 us; the launch traced here: 85.2 us
  Pallas kernels  79.3 us (93%)
  local copies, waits for them, and re-layouts  5.89 us (7%)
    pallas_call x1, Pallas kernels, shards(): pl.pallas_call(kernel, out_shape=jax.ShapeDtypeStruct((rows, targets), F3...  79.3 us
    unnamed x1, local copies, waits for them, and re-layouts  5.89 us

profile of v2, /device:TPU:0, one launch (start us, length us, event | category | flops | bytes accessed | tf_op | source)
XLA Modules:
  0.0 85.2 jit_solution(6494770833547690613)
XLA Ops:
  0.0 79.3 %shard_map.55 = f32[2048,768]{1,0:T(8,128)} custom-call(bf16[2048,768]{1,0:T(8,128)(2,1)} %y_hbm.1, bf16[2048,2048]{1,0:T(8,128)(2,1)} %vc_hbm.1, bf16[768,2048]{1,0:T(8,128)(2,1)} %vt_hbm.1, f32[1,256]{1,0:T(1,128)} %bitcast.2, f32[1,128]{1,0:T(1,128)} %bitcast.3), custom_call_target="tpu_custom_call" | custom-call | tf_op jit(solution)/shard_map/pallas_call | solution.py:329
  79.4 5.9 %copy.7 = f32[2048,768]{1,0:T(8,128)} copy(f32[2048,768]{1,0:T(8,128)} %shard_map.55) | data formatting | bytes 12582912

commit v3 on v2

--- a/solution.py
+++ b/solution.py
@@ -14,6 +14,8 @@
 SUM_DIMS = ((1, 2, 4), (2, 1, 4), (4, 1, 2))
 GATHER_DIMS = ((1, 2, 4), (2, 1, 4), (4, 2, 1))
 ROW_TILE = 512
+LAST_TILE = 256
+FAR = (3, 5, 6, 7)
 STEPS = (
     ("ps", 0, 2), ("tr", 6), ("tr", 5), ("tr", 2), ("ps", 0, 0), ("ps", 0, 1), ("pt", 0, 0), ("pc", 1, 0),
     ("ps", 1, 0), ("pt", 0, 1), ("pc", 1, 1), ("pc", 1, 2), ("ps", 1, 1), ("ps", 1, 2), ("tr", 3), ("tr", 0),
@@ -59,10 +61,11 @@
 
 
 def kernel(
-    y_hbm, vc_hbm, vt_hbm, lc_ref, lt_ref, out_hbm,
-    y, vc, vct, vt, vtt, acc, den, psend, precv, wown, qsend, qown, qrecv, q2send, q2recv, s, tbuf,
-    in_sem, out_sem, p_ss, p_rs, c_ss, c_rs, q_ss, q_rs, s_ss, s_rs, d_ss, d_rs, t_ss, t_rs,
+    y_hbm, vc_hbm, vt_hbm, lc_ref, lt_ref, acc0, acc1, acc2, tfar, vcfar,
+    y, vc, vct, vt, vtt, den, psend, precv, wown, qsend, qown, qrecv, q2send, q2recv, s, tbuf,
+    in_sem, p_ss, p_rs, c_ss, c_rs, q_ss, q_rs, s_ss, s_rs, d_ss, d_rs, t_ss, t_rs,
 ):
+    acc = (acc0, acc1, acc2)
     c, t = lax.axis_index("cmp"), lax.axis_index("tgt")
     rows, cols = y.shape[1], y.shape[2]
     kb = vc.shape[1] // 8
@@ -251,24 +254,23 @@
         t_copy(h, p, 3).wait_recv()
         t_copy(h, p, 7).start()
 
-    def o_copy(p, i):
-        start = pl.multiple_of(i * ROW_TILE, ROW_TILE)
-        return pltpu.make_async_copy(
-            acc.at[p, pl.ds(start, ROW_TILE)],
-            out_hbm.at[pl.ds(start, ROW_TILE), pl.ds(p * cols, cols)],
-            out_sem.at[p, i],
-        )
-
     per_half = CHUNKS // 2
 
     def acc_step(i, far, p):
         chunks = range(i * per_half, (i + 1) * per_half)
         group = (3, 5, 6, 7) if far else (0, 1, 2, 4)
-        first, last = not (i or far), i and far
         for h in chunks:
             for r in group:
                 if r >= 4:
                     t_copy(h, p, r).wait_recv()
+        if i and far:
+            for r in group:
+                n = FAR.index(block_of(GATHER_DIMS[p], r))
+                for h in chunks:
+                    at = pl.ds(n * half + (h - chunks[0]) * kcs, kcs)
+                    tfar[p, at, :] = tbuf[h, p, r]
+            return
+        first = not (i or far)
         rhs = jnp.concatenate([tbuf[h, p, r] for r in group for h in chunks], axis=0)
 
         @pl.loop(0, rows // ROW_TILE)
@@ -278,9 +280,7 @@
                 [vc[at, pl.ds(block_of(GATHER_DIMS[p], r) * kb + i * half, half)] for r in group], axis=1
             )
             prod = jnp.dot(lhs, rhs, preferred_element_type=F32)
-            acc[p, at, :] = prod if first else acc[p, at, :] + prod
-            if last:
-                o_copy(p, n).start()
+            acc[p][at, :] = prod if first else acc[p][at, :] + prod
 
     def setup():
         den[...] = (
@@ -289,6 +289,9 @@
         for copy in vt_in:
             copy.wait()
         vtt[...] = vt[...].T
+        for n, j in enumerate(FAR):
+            vc_in_far = vc[:, pl.ds(j * kb + half, half)]
+            vcfar[:, pl.ds(n * half, half)] = vc_in_far
 
     transpose(0, load_order)
     for p in range(PARTS):
@@ -313,9 +316,22 @@
             for p in range(PARTS):
                 p_copy(h, p, r).wait_send()
                 t_copy(h, p, r).wait_send()
-    for p in range(PARTS):
-        for i in range(rows // ROW_TILE):
-            o_copy(p, i).wait()
+
+
+def finish(acc0, acc1, acc2, tfar, vcfar, out_hbm, buf, sem):
+    acc = (acc0, acc1, acc2)
+    rows, cols = acc0.shape
+    copies = []
+    for n in range(rows // LAST_TILE):
+        at = pl.ds(n * LAST_TILE, LAST_TILE)
+        for p in range(PARTS):
+            prod = jnp.dot(vcfar[at, :], tfar[p], preferred_element_type=F32)
+            buf[at, pl.ds(p * cols, cols)] = acc[p][at, :] + prod
+        copy = pltpu.make_async_copy(buf.at[at], out_hbm.at[at], sem.at[n])
+        copy.start()
+        copies.append(copy)
+    for copy in copies:
+        copy.wait()
 
 
 def shards(affinity, comp_vectors, targ_vectors, comp_values, targ_values):
@@ -326,18 +342,21 @@
     any_space = pl.BlockSpec(memory_space=pl.ANY)
     vmem = pl.BlockSpec(memory_space=pltpu.VMEM)
     dma = pltpu.SemaphoreType.DMA
-    return pl.pallas_call(
+    partial = pl.pallas_call(
         kernel,
-        out_shape=jax.ShapeDtypeStruct((rows, targets), F32),
+        out_shape=[
+            *[jax.ShapeDtypeStruct((rows, cols), F32)] * PARTS,
+            jax.ShapeDtypeStruct((PARTS, 2 * kb, cols), BF16),
+            jax.ShapeDtypeStruct((rows, 2 * kb), BF16),
+        ],
         in_specs=[any_space, any_space, any_space, vmem, vmem],
-        out_specs=any_space,
+        out_specs=[vmem] * (PARTS + 2),
         scratch_shapes=[
             pltpu.VMEM((PARTS, rows, cols), BF16),
             pltpu.VMEM((rows, kc), BF16),
             pltpu.VMEM((kc, rows), BF16),
             pltpu.VMEM((targets, kt), BF16),
             pltpu.VMEM((kt, targets), BF16),
-            pltpu.VMEM((PARTS, rows, cols), F32),
             pltpu.VMEM((kb, tb), F32),
             pltpu.VMEM((n, PARTS, 7, kcs, cols), BF16),
             pltpu.VMEM((n, PARTS, 7, kcs, cols), BF16),
@@ -350,7 +369,6 @@
             pltpu.VMEM((n, 2, 8, kcs, tb), BF16),
             pltpu.VMEM((n, PARTS, 8, kcs, cols), BF16),
             dma((35,)),
-            dma((PARTS, rows // ROW_TILE)),
             dma((n, PARTS, 7)),
             dma((n, PARTS, 7)),
             dma((n,)),
@@ -365,9 +383,17 @@
             dma((n, PARTS, 7)),
         ],
         compiler_params=pltpu.CompilerParams(
-            collective_id=0, has_side_effects=True, vmem_limit_bytes=60 << 20
+            collective_id=0, has_side_effects=True, vmem_limit_bytes=45 << 20
         ),
     )(affinity, comp_vectors, targ_vectors, comp_values[None, :], targ_values[None, :])
+    return pl.pallas_call(
+        finish,
+        out_shape=jax.ShapeDtypeStruct((rows, targets), F32),
+        in_specs=[vmem] * (PARTS + 2),
+        out_specs=any_space,
+        scratch_shapes=[pltpu.VMEM((rows, targets), F32), dma((rows // LAST_TILE,))],
+        compiler_params=pltpu.CompilerParams(vmem_limit_bytes=8 << 20),
+    )(*partial)
 
 
 def solution(mesh):

time: 85.4 us -> 81.5 us (0.954)
  local copies, waits for them, and re-layouts: 5.89 us -> 1.33 us
    unnamed x1 -> x4, local copies, waits for them, and re-layouts: 5.89 us -> 1.33 us
    pallas_call x1 -> x2, Pallas kernels: 79.3 us -> 79.9 us  [the longest x1 76.7 us: shards(): pl.pallas_call(kernel, out_shape=[*[jax.ShapeDtypeStruct((rows, cols), F3...]
where the time goes in v3:
time: 81.5 us; the launch traced here: 81.4 us
  Pallas kernels  79.9 us (98%)
  local copies, waits for them, and re-layouts  1.33 us (2%)
    pallas_call x1, Pallas kernels, shards(): pl.pallas_call(kernel, out_shape=[*[jax.ShapeDtypeStruct((rows, cols), F3...  76.7 us
    pallas_call x1, Pallas kernels, shards(): pl.pallas_call(finish, out_shape=jax.ShapeDtypeStruct((rows, targets), F3...  3.19 us

profile of v3, /device:TPU:0, one launch (start us, length us, event | category | flops | bytes accessed | tf_op | source)
XLA Modules:
  0.0 81.4 jit_solution(16648657565091270946)
XLA Ops:
  0.0 0.0 copy-start
  0.0 0.7 copy-done
  0.7 0.0 copy-start.1
  0.7 0.7 copy-done.1
  1.3 76.7 %shard_map.55 = (f32[2048,256]{1,0:T(8,128)S(1)}, f32[2048,256]{1,0:T(8,128)S(1)}, f32[2048,256]{1,0:T(8,128)S(1)}, bf16[3,512,256]{2,1,0:T(8,128)(2,1)S(1)}, bf16[2048,512]{1,0:T(8,128)(2,1)S(1)}) custom-call(bf16[2048,768]{1,0:T(8,128)(2,1)} %y_hbm.1, bf16[2048,2048]{1,0:T(8,128)(2,1)} %vc_hbm.1, bf16[768,2048]{1,0:T(8,128)(2,1)} %vt_hbm.1, ...), custom_call_target="tpu_custom_call" | custom-call | tf_op jit(solution)/shard_map/pallas_call | solution.py:345
  78.0 3.2 %shard_map.56 = f32[2048,768]{1,0:T(8,128)} custom-call(f32[2048,256]{1,0:T(8,128)S(1)} %get-tuple-element.10.acc0, f32[2048,256]{1,0:T(8,128)S(1)} %get-tuple-element.11.acc1, f32[2048,256]{1,0:T(8,128)S(1)} %get-tuple-element.12.acc2, bf16[3,512,256]{2,1,0:T(8,128)(2,1)S(1)} %get-tuple-element.13.tfar, bf16[2048,512]{1,0:T(8,128)(2,1)S(1)} %get-tuple-element.14.vcfar), custom_call_target="tpu_custom_call" | custom-call | tf_op jit(solution)/shard_map/pallas_call | solution.py:389
Async XLA Ops:
  0.0 0.7 copy-start
  0.7 0.7 copy-start.1

commit v4 on v3

--- a/solution.py
+++ b/solution.py
@@ -17,22 +17,23 @@
 LAST_TILE = 256
 FAR = (3, 5, 6, 7)
 STEPS = (
-    ("ps", 0, 2), ("tr", 6), ("tr", 5), ("tr", 2), ("ps", 0, 0), ("ps", 0, 1), ("pt", 0, 0), ("pc", 1, 0),
-    ("ps", 1, 0), ("pt", 0, 1), ("pc", 1, 1), ("pc", 1, 2), ("ps", 1, 1), ("ps", 1, 2), ("tr", 3), ("tr", 0),
-    ("pt", 1, 2), ("p2", 0, 1), ("p2", 0, 0), ("tr", 1), ("tr", 4), ("tr", 7), ("pt", 1, 0), ("pt", 0, 2),
-    ("p2", 0, 2), ("pc", 3, 1), ("p2", 1, 0), ("pc", 2, 0), ("pt", 1, 1), ("p3", 0, 0), ("p3", 0, 1), ("p2", 1, 1),
-    ("p2", 1, 2), ("setup",), ("p3", 0, 2), ("pc", 3, 0), ("p3", 1, 0), ("ps", 3, 0), ("pt", 3, 0), ("ps", 3, 1),
-    ("p3", 1, 1), ("pc", 2, 1), ("ps", 2, 0), ("pc", 3, 2), ("ps", 3, 2), ("pt", 3, 2), ("p3", 1, 2), ("ps", 2, 1),
-    ("pf", 0), ("p2", 3, 0), ("pt", 2, 0), ("pc", 2, 2), ("ps", 2, 2), ("pt", 3, 1), ("m1", 0), ("p2", 3, 1),
-    ("pf", 1), ("p2", 2, 0), ("p2", 3, 2), ("pt", 2, 2), ("pt", 2, 1), ("m1", 1), ("p2", 2, 1), ("p3", 3, 0),
-    ("p3", 3, 1), ("m2", 0), ("p2", 2, 2), ("p3", 2, 0), ("p3", 3, 2), ("p3", 2, 1), ("m2", 1), ("m3", 0),
-    ("p3", 2, 2), ("pf", 3), ("m3", 1), ("m1", 3), ("m5", 0), ("pf", 2), ("m6", 0), ("m5", 1), ("m1", 2), ("m2", 3),
-    ("m6", 1), ("m2", 2), ("a1", 0, 0), ("a1", 0, 1), ("m3", 3), ("a1", 1, 0), ("m3", 2), ("a1", 0, 2), ("a1", 1, 1),
-    ("acc", 0, 0, 1), ("m5", 3), ("a1", 1, 2), ("a2", 0, 0), ("a2", 0, 1), ("a2", 1, 0), ("acc", 0, 0, 0),
-    ("a2", 1, 1), ("m6", 3), ("m5", 2), ("acc", 0, 0, 2), ("m6", 2), ("a2", 1, 2), ("a1", 3, 0), ("a2", 0, 2),
-    ("a1", 3, 2), ("acc", 0, 1, 0), ("acc", 0, 1, 1), ("a1", 2, 0), ("a1", 2, 2), ("a1", 3, 1), ("a1", 2, 1),
-    ("acc", 1, 0, 1), ("acc", 1, 0, 2), ("a2", 3, 0), ("a2", 3, 2), ("a2", 2, 0), ("a2", 2, 2), ("a2", 3, 1),
-    ("acc", 1, 0, 0), ("a2", 2, 1), ("acc", 0, 1, 2), ("acc", 1, 1, 0), ("acc", 1, 1, 2), ("acc", 1, 1, 1),)
+    ("ps", 0, 1), ("pc", 1, 1), ("ps", 0, 0), ("tr", 7), ("pt", 0, 0), ("ps", 1, 1), ("tr", 2), ("tr", 0),
+    ("pt", 1, 1), ("tr", 4), ("ps", 0, 2), ("tr", 3), ("tr", 6), ("pc", 1, 2), ("ps", 1, 2), ("p2", 0, 1),
+    ("pc", 1, 0), ("p2", 0, 0), ("pt", 0, 2), ("tr", 5), ("ps", 1, 0), ("tr", 1), ("pc", 3, 1), ("p2", 0, 2),
+    ("pt", 0, 1), ("pc", 3, 0), ("pt", 1, 2), ("ps", 3, 1), ("ps", 3, 0), ("pc", 2, 2), ("ps", 2, 2), ("p2", 1, 1),
+    ("p3", 0, 0), ("pt", 1, 0), ("pc", 2, 1), ("p2", 1, 0), ("p3", 0, 1), ("p2", 1, 2), ("pc", 3, 2), ("p3", 0, 2),
+    ("pc", 2, 0), ("ps", 3, 2), ("ps", 2, 0), ("pt", 3, 1), ("p3", 1, 1), ("pt", 3, 0), ("p3", 1, 0), ("p2", 3, 1),
+    ("setup",), ("p3", 1, 2), ("ps", 2, 1), ("pf", 0), ("pt", 2, 0), ("pt", 3, 2), ("pt", 2, 2), ("p2", 3, 0),
+    ("p2", 3, 2), ("p2", 2, 2), ("m1", 0), ("p3", 3, 1), ("p2", 2, 0), ("pf", 1), ("pt", 2, 1), ("p3", 3, 0),
+    ("p2", 2, 1), ("p3", 3, 2), ("m1", 1), ("m2", 0), ("p3", 2, 0), ("p3", 2, 1), ("p3", 2, 2), ("pf", 3), ("m3", 0),
+    ("m2", 1), ("m1", 3), ("pf", 2), ("m3", 1), ("m5", 0), ("m1", 2), ("m2", 3), ("m6", 0), ("m3", 3), ("m5", 1),
+    ("m2", 2), ("a1", 0, 0), ("m6", 1), ("a1", 0, 1), ("m5", 3), ("m3", 2), ("a2", 0, 0), ("a1", 0, 2), ("a1", 1, 2),
+    ("a1", 1, 0), ("m6", 3), ("m5", 2), ("a1", 1, 1), ("a2", 0, 1), ("acc", 0, 0, 0), ("a2", 1, 0), ("m6", 2),
+    ("a2", 1, 2), ("acc", 0, 0, 1), ("acc", 0, 0, 2), ("a1", 3, 2), ("a1", 3, 0), ("a2", 0, 2), ("acc", 0, 1, 0),
+    ("a1", 2, 2), ("a1", 2, 0), ("acc", 1, 0, 0), ("a2", 1, 1), ("a1", 2, 1), ("a1", 3, 1), ("a2", 3, 2),
+    ("acc", 1, 0, 2), ("a2", 3, 0), ("acc", 1, 0, 1), ("a2", 2, 2), ("a2", 2, 0), ("acc", 0, 1, 2), ("a2", 2, 1),
+    ("a2", 3, 1), ("acc", 0, 1, 1), ("acc", 1, 1, 0), ("acc", 1, 1, 2), ("acc", 1, 1, 1),
+)
 
 
 def flip4(v, bits):

time: 81.5 us -> 83.4 us (1.023)
  Pallas kernels: 79.9 us -> 81.8 us
    pallas_call x1, Pallas kernels: 76.7 us -> 78.6 us  [shards(): pl.pallas_call(kernel, out_shape=[*[jax.ShapeDtypeStruct((rows, cols), F3...]
where the time goes in v4:
time: 83.4 us; the launch traced here: 83.3 us
  Pallas kernels  81.8 us (98%)
  local copies, waits for them, and re-layouts  1.33 us (2%)
    pallas_call x1, Pallas kernels, shards(): pl.pallas_call(kernel, out_shape=[*[jax.ShapeDtypeStruct((rows, cols), F3...  78.6 us
    pallas_call x1, Pallas kernels, shards(): pl.pallas_call(finish, out_shape=jax.ShapeDtypeStruct((rows, targets), F3...  3.19 us

profile of v4, /device:TPU:0, one launch (start us, length us, event | category | flops | bytes accessed | tf_op | source)
XLA Modules:
  0.0 83.3 jit_solution(2433073438855562267)
XLA Ops:
  0.0 0.0 copy-start
  0.0 0.7 copy-done
  0.7 0.0 copy-start.1
  0.7 0.7 copy-done.1
  1.3 78.6 %shard_map.55 = (f32[2048,256]{1,0:T(8,128)S(1)}, f32[2048,256]{1,0:T(8,128)S(1)}, f32[2048,256]{1,0:T(8,128)S(1)}, bf16[3,512,256]{2,1,0:T(8,128)(2,1)S(1)}, bf16[2048,512]{1,0:T(8,128)(2,1)S(1)}) custom-call(bf16[2048,768]{1,0:T(8,128)(2,1)} %y_hbm.1, bf16[2048,2048]{1,0:T(8,128)(2,1)} %vc_hbm.1, bf16[768,2048]{1,0:T(8,128)(2,1)} %vt_hbm.1, ...), custom_call_target="tpu_custom_call" | custom-call | tf_op jit(solution)/shard_map/pallas_call | solution.py:346
  79.9 3.2 %shard_map.56 = f32[2048,768]{1,0:T(8,128)} custom-call(f32[2048,256]{1,0:T(8,128)S(1)} %get-tuple-element.10.acc0, f32[2048,256]{1,0:T(8,128)S(1)} %get-tuple-element.11.acc1, f32[2048,256]{1,0:T(8,128)S(1)} %get-tuple-element.12.acc2, bf16[3,512,256]{2,1,0:T(8,128)(2,1)S(1)} %get-tuple-element.13.tfar, bf16[2048,512]{1,0:T(8,128)(2,1)S(1)} %get-tuple-element.14.vcfar), custom_call_target="tpu_custom_call" | custom-call | tf_op jit(solution)/shard_map/pallas_call | solution.py:390
Async XLA Ops:
  0.0 0.7 copy-start
  0.7 0.7 copy-start.1
